TPU v7x, 128 devices: a whole 4x4x4 slice. The times are simulated.
128 devices in a mesh: dp: 16 (over x, z_hi, core), tm: 8 (over z_lo, y).
Axes of the slice: x: 4, y: 4, z: 4 (z_hi: 2, z_lo: 2; z = z_hi * 2 + z_lo), core: 2. Of those that a mesh axis runs over, the one named last changes fastest.
Arguments:
- loaded: bfloat16 [16, 64, 16, 16, 256], P('dp', 'tm')
- lengths: int32 [16, 8], P('dp'), may hold values from 1 to 8, as said below
- resolution: int32 [16, 2], P('dp'), may hold values from 8 to 16, as said below
- weight: bfloat16 [27, 256, 256], replicated, may hold values from -0.078125 to 0.078125
- norm_gain: float32 [256], replicated, may hold values from 0.1 to 1.9
- norm_bias: float32 [256], replicated, may hold values from -3 to 3
- cotangent: bfloat16 [16, 64, 16, 16, 256], P('dp', 'tm'), may hold values from -6 to 6
Outputs:
- encoded: bfloat16 [16, 64, 16, 16, 256], P('dp', 'tm')
- input_grad: bfloat16 [16, 64, 16, 16, 256], P('dp', 'tm')
- weight_grad: float32 [27, 256, 256], replicated
- gain_grad: float32 [256], replicated
- bias_grad: float32 [256], replicated
Inputs may be any that keep to these rules, and one draw needn't show every extreme that they name: `lengths`: row c lists how many consecutive frames of clip c each index of tm loaded, in frame order; the row sums to the clip's frame count, which is 64 - k for some 0 <= k <= 8, so that every loaded frame belongs to the loader's own temporal slab or to the one before it; in every draw one clip has all 64 frames, 8 on every index. `resolution`: valid rows (column 0) and columns (column 1) of clip c; frames are padded at the bottom and right; at least 8 rows and 8 columns, and in every draw one clip has the full 16 by 16.
All inputs are finite; a program needn't handle non-finite values.
Results may differ from a plain program's by a relative error of at most 0.0046.
The roundings to bfloat16 on the way count: a program that leaves them out, or rounds other values in their place, can miss the bound.
Values may be sent and summed in bfloat16 or wider, within the bound.
A program may use at most 128 MiB of HBM per device.

v0:
```python
import math
import jax
import jax.numpy as jnp
from jax import lax
from jax.sharding import PartitionSpec as P

GROUPS = 32
EPSILON = 1e-05


def shifted(block, axis, distance):
    devices = range(lax.axis_size(axis))
    route = [(i - distance, i) for i in devices if i - distance in devices]
    return lax.ppermute(block, axis, route)


def group_total(values):
    shaped = values.reshape(values.shape[:-1] + (GROUPS, values.shape[-1] // GROUPS))
    return jnp.sum(shaped, axis=(0, 1, 2, 4))


def spread_groups(per_group, channels):
    return jnp.repeat(per_group, channels // per_group.shape[0])


def tap_sweeps(past_pad, future_pad, weight, frames, frame_rows, frame_cols):
    channels = weight.shape[2]
    positions = frames * frame_rows * frame_cols
    forward = jnp.zeros((positions, channels), jnp.float32)
    backward = jnp.zeros((positions, channels), jnp.float32)
    grad_flat = future_pad[:frames, 1 : frame_rows + 1, 1 : frame_cols + 1].reshape(
        positions, channels
    )
    kernel_parts = []
    for time_tap in range(3):
        for row_tap in range(3):
            for col_tap in range(3):
                tap_index = time_tap * 9 + row_tap * 3 + col_tap
                past_slice = past_pad[
                    time_tap : time_tap + frames,
                    row_tap : row_tap + frame_rows,
                    col_tap : col_tap + frame_cols,
                ].reshape(positions, channels)
                forward = forward + jnp.dot(
                    past_slice, weight[tap_index], preferred_element_type=jnp.float32
                )
                kernel_parts.append(
                    lax.dot_general(
                        past_slice,
                        grad_flat,
                        (((0,), (0,)), ((), ())),
                        preferred_element_type=jnp.float32,
                    )
                )
                future_slice = future_pad[
                    2 - time_tap : 2 - time_tap + frames,
                    2 - row_tap : 2 - row_tap + frame_rows,
                    2 - col_tap : 2 - col_tap + frame_cols,
                ].reshape(positions, channels)
                backward = backward + lax.dot_general(
                    future_slice,
                    weight[tap_index],
                    (((1,), (1,)), ((), ())),
                    preferred_element_type=jnp.float32,
                )
    return (forward, backward, jnp.stack(kernel_parts))


def place_frames(own_frames, slab_start, first_frame, own_length):
    frames = own_frames.shape[0]
    offset = slab_start + jnp.arange(frames, dtype=jnp.int32) - first_frame
    usable = (offset >= 0) & (offset < own_length)
    picked = jnp.take(own_frames, jnp.clip(offset, 0, frames - 1), axis=0)
    return picked * usable.astype(jnp.bfloat16)[:, None, None, None]


def body(loaded, lengths, resolution, weight, norm_gain, norm_bias, cotangent):
    own_frames = loaded[0]
    frames, frame_rows, frame_cols, channels = own_frames.shape
    slab_count = lax.axis_size("tm")
    own_slab = lax.axis_index("tm")
    length_row = lengths[0]
    starts = jnp.cumsum(length_row) - length_row
    frame_total = jnp.sum(length_row)
    first_frame = starts[own_slab]
    own_length = length_row[own_slab]
    staying = place_frames(own_frames, own_slab * frames, first_frame, own_length)
    leaving = place_frames(own_frames, (own_slab - 1) * frames, first_frame, own_length)
    arrived = shifted(leaving, "tm", -1)
    assembled = staying.astype(jnp.float32) + arrived.astype(jnp.float32)
    frame_ids = own_slab * frames + jnp.arange(frames, dtype=jnp.int32)
    live_rows = jnp.arange(frame_rows, dtype=jnp.int32) < resolution[0, 0]
    live_cols = jnp.arange(frame_cols, dtype=jnp.int32) < resolution[0, 1]
    live_cells = (
        (frame_ids < frame_total)[:, None, None]
        & live_rows[None, :, None]
        & live_cols[None, None, :]
    ).astype(jnp.float32)[..., None]
    inputs_f = assembled * live_cells
    cell_count = (frame_total * resolution[0, 0] * resolution[0, 1] * (channels // GROUPS)).astype(
        jnp.float32
    )
    group_means = lax.psum(group_total(inputs_f), "tm") / cell_count
    centred = (inputs_f - spread_groups(group_means, channels)) * live_cells
    variance = lax.psum(group_total(centred * centred), "tm") / cell_count
    inverse_root = spread_groups(lax.rsqrt(variance + EPSILON), channels)
    normed = centred * inverse_root
    pre_activation = normed * norm_gain + norm_bias
    gate_value = jax.nn.sigmoid(pre_activation)
    activation = (pre_activation * gate_value * live_cells).astype(jnp.bfloat16)
    earlier = shifted(activation[frames - 2 :], "tm", 1)
    past_pad = jnp.pad(
        jnp.concatenate([earlier, activation], axis=0), ((0, 0), (1, 1), (1, 1), (0, 0))
    )
    masked_grad = cotangent[0] * live_cells.astype(jnp.bfloat16)
    future = shifted(masked_grad[:2], "tm", -1)
    future_pad = jnp.pad(
        jnp.concatenate([masked_grad, future], axis=0), ((0, 0), (1, 1), (1, 1), (0, 0))
    )
    forward, backward, kernel_part = tap_sweeps(
        past_pad, future_pad, weight, frames, frame_rows, frame_cols
    )
    encoded = (forward.reshape(frames, frame_rows, frame_cols, channels) * live_cells).astype(
        jnp.bfloat16
    )
    activation_grad = backward.reshape(frames, frame_rows, frame_cols, channels) * live_cells
    pre_grad = activation_grad * gate_value * (1.0 + pre_activation * (1.0 - gate_value))
    gain_part = jnp.sum(pre_grad * normed, axis=(0, 1, 2))
    bias_part = jnp.sum(pre_grad, axis=(0, 1, 2))
    normed_grad = pre_grad * norm_gain
    normed_sum, projected_sum = lax.psum(
        (group_total(normed_grad), group_total(normed_grad * normed)), "tm"
    )
    grad_mean = spread_groups(normed_sum / cell_count, channels)
    grad_proj = spread_groups(projected_sum / cell_count, channels)
    input_grad = (
        inverse_root * (normed_grad - grad_mean - normed * grad_proj) * live_cells
    ).astype(jnp.bfloat16)
    kernel_sum, gain_sum, bias_sum = lax.psum((kernel_part, gain_part, bias_part), ("dp", "tm"))
    grad_scale = 1.0 / math.sqrt(
        lax.axis_size("dp") * slab_count * frames * frame_rows * frame_cols
    )
    return (
        encoded[None],
        input_grad[None],
        kernel_sum * grad_scale,
        gain_sum * grad_scale,
        bias_sum * grad_scale,
    )


def solution(mesh):
    placed = (
        P("dp", "tm", None, None, None),
        P("dp", None),
        P("dp", None),
        P(),
        P(),
        P(),
        P("dp", "tm", None, None, None),
    )
    return jax.shard_map(
        body,
        mesh=mesh,
        in_specs=placed,
        out_specs=(P("dp", "tm", None, None, None), P("dp", "tm", None, None, None), P(), P(), P()),
        check_vma=False,
    )
```

profile of v0, /device:TPU:1, one launch (start us, length us, event | category | flops | bytes accessed | tf_op | source)
XLA Modules:
  0.0 453.0 jit_solution(18382396377118999737)
XLA Ops:
  7.2 0.9 reduce-window.9
  8.8 1.2 constant_dynamic-slice_fusion
  10.6 1.3 compare_and_fusion
  12.6 1.1 select_multiply_fusion
  13.7 1.3 collective-permute-start
  19.5 1.3 collective-permute-start.2
  20.8 1.3 compare_and_fusion.1
  24.6 2.5 broadcast_multiply_fusion.1
  27.2 18.9 %collective-permute-done.2 = bf16[2,16,16,256]{3,2,1,0:T(8,128)(2,1)S(1)} collective-permute-done((bf16[2,16,16,256]{3,2,1,0:T(8,128)(2,1)}, bf16[2,16,16,256]{3,2,1,0:T(8,128)(2,1)S(1)}, u32[]{:S(2)}, u32[]{:S(2)}) %collective-permute-start.2) | collective-permute-done | bytes 262176 | tf_op jit(solution)/shard_map/ppermute | solution.py:14
  46.2 7.1 %pad_slice_fusion = (bf16[8,16,16,256]{3,2,1,0:T(8,128)(2,1)}, bf16[8,16,16,256]{3,2,1,0:T(8,128)(2,1)}, bf16[8,16,16,256]{3,2,1,0:T(8,128)(2,1)}, bf16[8,16,16,...) fusion(bf16[10,16,16,256]{3,2,1,0:T(8,128)(2,1)S(1)} %pad_maxim, ...), kind=kLoop, calls=%fused_computation.2 | loop fusion | bytes 21233664 | tf_op jit(solution)/shard_map/slice | solution.py:55
  53.3 2.4 pad_slice_fusion.1
  82.5 1.8 convolution_add_fusion
  84.3 1.8 fusion
  86.3 15.2 %psum.49 = f32[32]{0:T(128)S(1)} all-reduce(f32[32]{0:T(128)S(1)} %reduce_sum.76), channel_id=1, replica_groups=mesh['dp'=16,'tm'=8] {'tm'}, use_global_device_ids=true, to_apply=%region_4.6 | all-reduce | flops 32 | bytes 256 | tf_op jit(solution)/shard_map/psum | solution.py:103
  101.7 2.0 multiply_reduce_fusion.2
  103.9 25.4 %psum.50 = f32[32]{0:T(128)S(1)} all-reduce(f32[32]{0:T(128)S(1)} %reduce_sum.97), channel_id=1, replica_groups=mesh['dp'=16,'tm'=8] {'tm'}, use_global_device_ids=true, to_apply=%region_7.9 | all-reduce | flops 32 | bytes 256 | tf_op jit(solution)/shard_map/psum | solution.py:105
  129.4 4.7 %multiply_reduce_fusion = (f32[256]{0:T(256)S(1)}, f32[256]{0:T(256)S(1)}, f32[256]{0:T(256)S(1)}, f32[256]{0:T(256)S(1)}, f32[8,16,16,256]{3,2,1,0:T(8,128)}, /*index=5*/bf16[8,16,16,256]{3,2,1,0:T(8,128)(2,1)S(1)}) fusion(f32[256]{0:T(256)S(1)} %mul.181, f32[256]{0:T(256)S(1)} %sub.55, f32[8,16,16]{2,1,0:T(8,128)S(1)} %get-tuple-element.73, ...), kind=kLoop, calls=%fused_computation.103 | loop fusion | flops 15727616 | bytes 7356440 | tf_op jit(solution)/shard_map/reduce_sum | solution.py:128
  134.9 2.9 collective-permute-start.1
  138.2 15.0 %all-reduce.3 = (f32[32]{0:T(128)S(1)}, f32[32]{0:T(128)S(1)}) all-reduce(f32[32]{0:T(128)S(1)} %reduce_sum.103, f32[32]{0:T(128)S(1)} %reduce_sum.100), channel_id=1, replica_groups=mesh['dp'=16,'tm'=8] {'tm'}, use_global_device_ids=true, to_apply=%region_13.15 | all-reduce | flops 64 | bytes 512 | tf_op jit(solution)/shard_map/psum | solution.py:131
  153.6 80.1 %all-reduce.2 = (f32[256]{0:T(256)S(1)}, f32[256]{0:T(256)S(1)}) all-reduce(f32[256]{0:T(256)S(1)} %get-tuple-element.6, f32[256]{0:T(256)S(1)} %get-tuple-element.9), channel_id=1, replica_groups=mesh['dp'=16,'tm'=8] {'dp','tm'}, use_global_device_ids=true, to_apply=%region_16.18 | all-reduce | flops 512 | bytes 4096 | tf_op jit(solution)/shard_map/psum | solution.py:139
  233.6 3.9 fusion.33
  238.8 7.0 %pad_slice_fusion.24 = (bf16[8,16,16,256]{3,2,1,0:T(8,128)(2,1)}, bf16[8,16,16,256]{3,2,1,0:T(8,128)(2,1)S(1)}, bf16[8,16,16,256]{3,2,1,0:T(8,128)(2,1)}, bf16[8...) fusion(bf16[10,16,16,256]{3,2,1,0:T(8,128)(2,1)S(1)} %pad_maxim, ...), kind=kLoop, calls=%fused_computation.26 | loop fusion | bytes 21233664 | tf_op jit(solution)/shard_map/slice | solution.py:39
  245.8 2.7 pad_slice_fusion.25
  248.5 1.2 fusion.28
  249.7 2.7 fusion.86
  252.4 1.2 fusion.27
  253.6 1.2 fusion.26
  254.8 1.2 fusion.25
  256.0 1.2 fusion.3
  257.2 1.2 fusion.24
  258.4 1.2 fusion.23
  259.6 1.2 fusion.22
  260.8 1.2 fusion.21
  262.0 1.2 fusion.20
  263.2 1.2 fusion.19
  264.4 1.2 fusion.18
  265.6 1.2 fusion.17
  266.8 1.2 fusion.2
  267.9 1.2 fusion.16
  269.1 1.2 fusion.15
  270.3 1.2 fusion.14
  271.6 1.2 fusion.13
  272.8 1.2 fusion.12
  273.9 1.2 fusion.11
  275.1 1.2 fusion.10
  276.3 1.2 fusion.9
  277.5 1.2 fusion.8
  278.7 1.2 fusion.7
  279.9 1.2 fusion.6
  281.1 1.2 fusion.5
  282.3 1.2 fusion.4
  283.5 1.2 copy-done.8
  284.8 2.2 convolution_add_fusion.51
  288.2 1.1 copy-done.27
  293.0 0.8 copy-done.24
  297.9 0.8 copy-done.20
  299.2 0.8 copy-done.19
  302.2 0.8 copy-done.17
  305.9 0.8 copy-done.14
  307.2 0.8 copy-done.13
  309.6 0.8 copy-done.7
  315.6 1.3 multiply_convert_fusion.1
  316.9 122.3 %all-reduce.6.cloned.1.call-done = f32[27,256,256]{2,1,0:T(8,128)} async-done(((f32[27,256,256]{2,1,0:T(8,128)}), f32[27,256,256]{2,1,0:T(8,128)}) %all-reduce.6.cloned.1.call-update) | async-done | bytes 7077904 | tf_op jit(solution)/shard_map/psum | solution.py:139
  439.2 6.8 %broadcast_multiply_fusion = f32[27,256,256]{2,1,0:T(8,128)} fusion(f32[27,256,256]{2,1,0:T(8,128)} %all-reduce.6.cloned.1.call-done), kind=kLoop, calls=%fused_computation.50 | loop fusion | flops 1769472 | bytes 14155776 | tf_op jit(solution)/shard_map/mul | solution.py:146
  (190 shorter events, 58.6 us)
Async XLA Ops:
  7.2 4.8 %copy-start = (bf16[1,8,16,16,256]{4,3,2,1,0:T(8,128)(2,1)S(1)}, bf16[1,8,16,16,256]{4,3,2,1,0:T(8,128)(2,1)}, u32[]{:S(2)}) copy-start(bf16[1,8,16,16,256]{4,3,2,1,0:T(8,128)(2,1)} %param.9) | copy-start | bytes 3145732
  7.2 432.0 %all-reduce.6.cloned.1.call-start = ((), (), s32[]{:S(2)}) async-start(), calls=%async_computation | async-start | bytes 14155776 | tf_op jit(solution)/shard_map/psum | solution.py:139
  11.9 3.1 copy-start.50
  12.0 3.7 copy-start.48
  12.0 6.5 %copy-start.4 = (bf16[1,8,16,16,256]{4,3,2,1,0:T(8,128)(2,1)S(1)}, bf16[1,8,16,16,256]{4,3,2,1,0:T(8,128)(2,1)}, u32[]{:S(2)}) copy-start(bf16[1,8,16,16,256]{4,3,2,1,0:T(8,128)(2,1)} %param.15) | copy-start | bytes 3145732
  13.7 70.5 %collective-permute-start = (bf16[8,16,16,256]{3,2,1,0:T(8,128)(2,1)}, bf16[8,16,16,256]{3,2,1,0:T(8,128)(2,1)}, u32[]{:S(2)}, u32[]{:S(2)}) collective-permute-start(bf16[8,16,16,256]{3,2,1,0:T(8,128)(2,1)} %select_multiply_fusion), channel_id=1, source_target_pairs={{1,0},{2,1},{3,2},{4,3},{5,4},{6,5},{7,6},{9,8},{10,9},{11,10},{12... | collective-permute-start | bytes 3145736 | tf_op jit(solution)/shard_map/ppermute | solution.py:14
  19.5 26.6 %collective-permute-start.2 = (bf16[2,16,16,256]{3,2,1,0:T(8,128)(2,1)}, bf16[2,16,16,256]{3,2,1,0:T(8,128)(2,1)S(1)}, u32[]{:S(2)}, u32[]{:S(2)}) collective-permute-start(bf16[2,16,16,256]{3,2,1,0:T(8,128)(2,1)} %slice.379), channel_id=1, source_target_pairs={{1,0},{2,1},{3,2},{4,3},{5,4},{6,5},{7,6},{9,8},{10,9},{11,10},{12... | collective-permute-start | bytes 786440 | tf_op jit(solution)/shard_map/ppermute | solution.py:14
  53.3 2.4 copy-start.2
  53.3 2.4 copy-start.10
  56.2 1.2 copy-start.46
  57.4 1.2 copy-start.45
  59.3 1.2 copy-start.44
  60.5 1.2 copy-start.43
  61.7 1.2 copy-start.42
  62.9 1.2 copy-start.41
  64.2 1.2 copy-start.40
  65.4 1.2 copy-start.39
  66.6 1.2 copy-start.38
  67.8 1.2 copy-start.37
  69.5 1.2 copy-start.36
  70.8 1.2 copy-start.35
  72.0 1.2 copy-start.34
  73.2 1.2 copy-start.33
  74.4 1.2 copy-start.32
  75.7 1.2 copy-start.31
  76.9 1.2 copy-start.30
  78.6 1.2 copy-start.9
  81.3 1.2 copy-start.29
  84.3 45.1 %copy-start.47 = (f32[256]{0:T(256)S(1)}, f32[256]{0:T(256)}, u32[]{:S(2)}) copy-start(f32[256]{0:T(256)} %param.13) | copy-start | bytes 3076
  84.3 45.1 %copy-start.49 = (f32[256]{0:T(256)S(1)}, f32[256]{0:T(256)}, u32[]{:S(2)}) copy-start(f32[256]{0:T(256)} %param.14) | copy-start | bytes 3076
  134.9 103.9 %collective-permute-start.1 = (bf16[2,16,16,256]{3,2,1,0:T(8,128)(2,1)}, bf16[2,16,16,256]{3,2,1,0:T(8,128)(2,1)S(1)}, u32[]{:S(2)}, u32[]{:S(2)}) collective-permute-start(bf16[2,16,16,256]{3,2,1,0:T(8,128)(2,1)} %slice.374), channel_id=1, source_target_pairs={{0,1},{1,2},{2,3},{3,4},{4,5},{5,6},{6,7},{8,9},{9,10},{10,11},{11... | collective-permute-start | bytes 786440 | tf_op jit(solution)/shard_map/ppermute | solution.py:14
  283.5 1.2 copy-start.8
  284.7 2.7 copy-start.3
  284.7 3.0 copy-start.28
  287.7 1.5 copy-start.27
  290.1 1.2 copy-start.26
  291.3 1.2 copy-start.25
  292.5 1.3 copy-start.24
  293.8 1.3 copy-start.23
  295.0 1.2 copy-start.22
  296.3 1.2 copy-start.21
  297.5 1.3 copy-start.20
  298.8 1.3 copy-start.19
  300.5 1.3 copy-start.18
  301.7 1.3 copy-start.17
  303.0 1.2 copy-start.16
  304.2 1.2 copy-start.15
  305.4 1.3 copy-start.14
  306.7 1.3 copy-start.13
  308.0 1.2 copy-start.12
  309.2 1.3 copy-start.7
  310.9 1.3 copy-start.6
  312.2 1.3 copy-start.5
  313.9 1.3 copy-start.11
  439.2 6.8 %copy-start.1 = (bf16[1,8,16,16,256]{4,3,2,1,0:T(8,128)(2,1)S(1)}, bf16[1,8,16,16,256]{4,3,2,1,0:T(8,128)(2,1)}, u32[]{:S(2)}) copy-start(bf16[1,8,16,16,256]{4,3,2,1,0:T(8,128)(2,1)} %param.9) | copy-start | bytes 3145732
Sparse Core Ops, SparseCore 0:
  283.7 155.4 all-reduce.5
where the time goes:
time: 458 us; the launch traced here: 453 us
  waiting for transfers between devices  141 us (31%)
  blocking collectives  136 us (30%)
  matrix products  62.2 us (14%)
  local copies, waits for them, and re-layouts  58 us (13%)
  other arithmetic  33.6 us (7%)
  between operations  16.9 us (4%)
  starting transfers between devices  5.49 us (1%)
    psum x1, waiting for transfers between devices, body(): lax.psum((kernel_part, gain_part, bias_part), ('dp', 'tm'))  122 us
    psum x1, blocking collectives, body(): lax.psum((kernel_part, gain_part, bias_part), ('dp', 'tm'))  80.1 us
    unnamed x102, local copies, waits for them, and re-layouts  32.7 us
    dot_general x27, matrix products, tap_sweeps(): lax.dot_general(past_slice, grad_flat, (((0,), (0,)), ((), ())), preferre...  32.2 us
    psum x1, blocking collectives, body(): variance = lax.psum(group_total(centred * centred), 'tm') / cell_count  25.4 us
    ppermute x3, waiting for transfers between devices, shifted(): return lax.ppermute(block, axis, route)  18.9 us
    dot_general x27, matrix products, tap_sweeps(): jnp.dot(past_slice, weight[tap_index], preferred_element_type=jnp.float32)  16 us
    psum x1, blocking collectives, body(): group_means = lax.psum(group_total(inputs_f), 'tm') / cell_count  15.2 us
  transfers between devices with their start and end apart: 4, of which 2 were waited for; matrix products, arithmetic and copies ran while one was open for 12% of the time, Pallas kernels for 0%

commit v1 on v0

--- a/solution.py
+++ b/solution.py
@@ -6,6 +6,11 @@
 
 GROUPS = 32
 EPSILON = 1e-05
+
+
+def one_after_other(array, one, other):
+    half = lax.psum(array, one)
+    return lax.psum(half, other)
 
 
 def shifted(block, axis, distance):
@@ -136,7 +141,9 @@
     input_grad = (
         inverse_root * (normed_grad - grad_mean - normed * grad_proj) * live_cells
     ).astype(jnp.bfloat16)
-    kernel_sum, gain_sum, bias_sum = lax.psum((kernel_part, gain_part, bias_part), ("dp", "tm"))
+    kernel_sum, gain_sum, bias_sum = one_after_other(
+        (kernel_part, gain_part, bias_part), "tm", "dp"
+    )
     grad_scale = 1.0 / math.sqrt(
         lax.axis_size("dp") * slab_count * frames * frame_rows * frame_cols
     )

time: 458 us -> 535 us (1.17)
  waiting for transfers between devices: 141 us -> 218 us
  local copies, waits for them, and re-layouts: 58 us -> 51.7 us
    psum x1 -> x2, waiting for transfers between devices: 122 us -> 195 us  [the longest x1 158 us: one_after_other(): return lax.psum(half, other)]
    psum x1, blocking collectives: 25.4 us -> 12.5 us  [body(): variance = lax.psum(group_total(centred * centred), 'tm') / cell_count]
    psum x1, blocking collectives: 80.1 us -> 92 us  [one_after_other(): return lax.psum(half, other)]
    unnamed x102 -> x108, local copies, waits for them, and re-layouts: 32.7 us -> 27.1 us
  transfers between devices with their start and end apart: 4 -> 5, of which waited for: 2 -> 4; matrix products, arithmetic and copies ran while one was open for 12% -> 13% of each run, Pallas kernels for 0% -> 0%
where the time goes in v1:
time: 535 us; the launch traced here: 529 us
  waiting for transfers between devices  218 us (41%)
  blocking collectives  136 us (25%)
  matrix products  66.7 us (12%)
  local copies, waits for them, and re-layouts  51.7 us (10%)
  other arithmetic  33.8 us (6%)
  between operations  17 us (3%)
  starting transfers between devices  6.14 us (1%)
    psum x1, waiting for transfers between devices, one_after_other(): return lax.psum(half, other)  158 us
    psum x1, blocking collectives, one_after_other(): return lax.psum(half, other)  92 us
    psum x1, waiting for transfers between devices, one_after_other(): half = lax.psum(array, one)  37.5 us
    dot_general x27, matrix products, tap_sweeps(): lax.dot_general(past_slice, grad_flat, (((0,), (0,)), ((), ())), preferre...  32 us
    unnamed x108, local copies, waits for them, and re-layouts  27.1 us
    ppermute x3, waiting for transfers between devices, shifted(): return lax.ppermute(block, axis, route)  22.9 us
    dot_general x27, matrix products, tap_sweeps(): jnp.dot(past_slice, weight[tap_index], preferred_element_type=jnp.float32)  20.8 us
    psum x1, blocking collectives, body(): lax.psum((group_total(normed_grad), group_total(normed_grad * normed)), '...  16.2 us
  transfers between devices with their start and end apart: 5, of which 4 were waited for; matrix products, arithmetic and copies ran while one was open for 13% of the time, Pallas kernels for 0%

profile of v1, /device:TPU:1, one launch (start us, length us, event | category | flops | bytes accessed | tf_op | source)
XLA Modules:
  0.0 529.4 jit_solution(5921603355026780784)
XLA Ops:
  8.8 1.2 constant_dynamic-slice_fusion
  10.6 1.3 compare_and_fusion
  12.6 1.1 select_multiply_fusion
  13.7 1.3 collective-permute-start
  19.5 1.3 collective-permute-start.2
  20.8 1.3 compare_and_fusion.1
  24.7 1.6 broadcast_multiply_fusion.1
  26.2 19.8 %collective-permute-done.2 = bf16[2,16,16,256]{3,2,1,0:T(8,128)(2,1)S(1)} collective-permute-done((bf16[2,16,16,256]{3,2,1,0:T(8,128)(2,1)}, bf16[2,16,16,256]{3,2,1,0:T(8,128)(2,1)S(1)}, u32[]{:S(2)}, u32[]{:S(2)}) %collective-permute-start.2) | collective-permute-done | bytes 262176 | tf_op jit(solution)/shard_map/ppermute | solution.py:19
  46.2 7.1 %pad_slice_fusion = (bf16[8,16,16,256]{3,2,1,0:T(8,128)(2,1)}, bf16[8,16,16,256]{3,2,1,0:T(8,128)(2,1)}, bf16[8,16,16,256]{3,2,1,0:T(8,128)(2,1)}, bf16[8,16,16,...) fusion(bf16[10,16,16,256]{3,2,1,0:T(8,128)(2,1)S(1)} %pad_maxim, ...), kind=kLoop, calls=%fused_computation.2 | loop fusion | bytes 21233664 | tf_op jit(solution)/shard_map/slice | solution.py:60
  53.3 2.5 pad_slice_fusion.1
  81.8 1.8 convolution_add_fusion
  83.6 1.8 fusion
  85.6 15.2 %psum.70 = f32[32]{0:T(128)S(1)} all-reduce(f32[32]{0:T(128)S(1)} %reduce_sum.76), channel_id=1, replica_groups=mesh['dp'=16,'tm'=8] {'tm'}, use_global_device_ids=true, to_apply=%region_4.6 | all-reduce | flops 32 | bytes 256 | tf_op jit(solution)/shard_map/psum | solution.py:108
  101.0 2.0 multiply_reduce_fusion.2
  103.2 12.5 %psum.71 = f32[32]{0:T(128)S(1)} all-reduce(f32[32]{0:T(128)S(1)} %reduce_sum.97), channel_id=1, replica_groups=mesh['dp'=16,'tm'=8] {'tm'}, use_global_device_ids=true, to_apply=%region_7.9 | all-reduce | flops 32 | bytes 256 | tf_op jit(solution)/shard_map/psum | solution.py:110
  115.9 4.8 multiply_reduce_fusion
  120.7 3.5 collective-permute-start.1
  124.2 3.1 collective-permute-done.1
  127.5 1.2 fusion.28
  128.7 1.2 fusion.27
  129.8 1.2 fusion.26
  131.0 1.2 fusion.25
  132.2 1.2 fusion.3
  133.4 1.2 fusion.24
  134.6 1.2 fusion.23
  135.7 1.2 fusion.22
  136.9 1.2 fusion.21
  138.1 1.2 fusion.20
  139.3 1.2 fusion.19
  140.5 1.2 fusion.18
  141.7 1.2 fusion.17
  142.9 1.2 fusion.2
  144.0 1.2 fusion.16
  145.2 1.2 fusion.15
  146.4 1.2 fusion.14
  147.6 1.2 fusion.13
  148.8 1.2 fusion.12
  150.0 1.2 fusion.11
  151.2 1.2 fusion.10
  152.3 1.2 fusion.9
  153.5 1.2 fusion.8
  154.7 1.2 fusion.7
  155.9 1.2 fusion.6
  157.1 1.2 fusion.5
  158.3 1.2 fusion.4
  159.9 16.2 %all-reduce.3 = (f32[32]{0:T(128)S(1)}, f32[32]{0:T(128)S(1)}, f32[256]{0:T(256)S(1)}, f32[256]{0:T(256)S(1)}) all-reduce(f32[32]{0:T(128)S(1)} %reduce_sum.103, f32[32]{0:T(128)S(1)} %reduce_sum.100, f32[256]{0:T(256)S(1)} %get-tuple-element.6, f32[256]{0:T(256)S(1)} %get-tuple-element.9), channel_id=1, replica_groups=mesh['dp'=16,'tm'=8] {'tm'}, use_global_device_ids=true, to_apply=%region_13.15 | all-reduce | flops 576 | bytes 4608 | tf_op jit(solution)/shard_map/psum | solution.py:136
  176.5 92.0 %all-reduce.2 = (f32[256]{0:T(256)S(1)}, f32[256]{0:T(256)S(1)}) all-reduce(f32[256]{0:T(256)S(1)} %get-tuple-element.14, f32[256]{0:T(256)S(1)} %get-tuple-element.15), channel_id=1, replica_groups=mesh['dp'=16,'tm'=8] {'dp'}, use_global_device_ids=true, to_apply=%region_18.20 | all-reduce | flops 512 | bytes 4096 | tf_op jit(solution)/shard_map/psum | solution.py:13
  269.6 4.0 fusion.33
  273.6 1.1 fusion.32
  274.7 2.8 pad_slice_fusion.25
  277.5 6.9 %pad_slice_fusion.24 = (bf16[8,16,16,256]{3,2,1,0:T(8,128)(2,1)}, bf16[8,16,16,256]{3,2,1,0:T(8,128)(2,1)S(1)}, bf16[8,16,16,256]{3,2,1,0:T(8,128)(2,1)}, bf16[8...) fusion(bf16[10,16,16,256]{3,2,1,0:T(8,128)(2,1)S(1)} %pad_maxim, ...), kind=kLoop, calls=%fused_computation.26 | loop fusion | bytes 21233664 | tf_op jit(solution)/shard_map/slice | solution.py:44
  284.5 1.3 fusion.86
  285.8 1.5 convolution_add_fusion.51
  287.3 1.4 convolution_add_fusion.50
  288.7 1.3 convolution_add_fusion.49
  290.1 1.4 convolution_add_fusion.48
  291.6 1.4 convolution_add_fusion.47
  293.0 1.4 convolution_add_fusion.46
  294.5 1.3 convolution_add_fusion.45
  295.8 37.5 %all-reduce.7.cloned.1.call-done = f32[27,256,256]{2,1,0:T(8,128)} async-done(((f32[27,256,256]{2,1,0:T(8,128)}), f32[27,256,256]{2,1,0:T(8,128)}) %all-reduce.7.cloned.1.call-update) | async-done | bytes 7077904 | tf_op jit(solution)/shard_map/psum | solution.py:12
  333.3 1.8 convolution_add_fusion.44
  356.5 1.3 multiply_convert_fusion.1
  357.8 157.7 %all-reduce.9.cloned.1.call-done = f32[27,256,256]{2,1,0:T(8,128)} async-done(((f32[27,256,256]{2,1,0:T(8,128)}), f32[27,256,256]{2,1,0:T(8,128)}) %all-reduce.9.cloned.1.call-update) | async-done | bytes 7077904 | tf_op jit(solution)/shard_map/psum | solution.py:13
  515.6 6.8 %broadcast_multiply_fusion = f32[27,256,256]{2,1,0:T(8,128)} fusion(f32[27,256,256]{2,1,0:T(8,128)} %all-reduce.9.cloned.1.call-done), kind=kLoop, calls=%fused_computation.50 | loop fusion | flops 1769472 | bytes 14155776 | tf_op jit(solution)/shard_map/mul | solution.py:153
  (199 shorter events, 58.0 us)
Async XLA Ops:
  7.2 4.8 copy-start
  7.2 326.1 %all-reduce.7.cloned.1.call-start = ((), (), s32[]{:S(2)}) async-start(), calls=%async_computation | async-start | bytes 14155776 | tf_op jit(solution)/shard_map/psum | solution.py:12
  11.9 3.1 copy-start.53
  12.0 3.8 copy-start.51
  12.0 6.5 %copy-start.6 = (bf16[1,8,16,16,256]{4,3,2,1,0:T(8,128)(2,1)S(1)}, bf16[1,8,16,16,256]{4,3,2,1,0:T(8,128)(2,1)}, u32[]{:S(2)}) copy-start(bf16[1,8,16,16,256]{4,3,2,1,0:T(8,128)(2,1)} %param.15) | copy-start | bytes 3145732
  13.7 69.9 %collective-permute-start = (bf16[8,16,16,256]{3,2,1,0:T(8,128)(2,1)}, bf16[8,16,16,256]{3,2,1,0:T(8,128)(2,1)}, u32[]{:S(2)}, u32[]{:S(2)}) collective-permute-start(bf16[8,16,16,256]{3,2,1,0:T(8,128)(2,1)} %select_multiply_fusion), channel_id=1, source_target_pairs={{1,0},{2,1},{3,2},{4,3},{5,4},{6,5},{7,6},{9,8},{10,9},{11,10},{12... | collective-permute-start | bytes 3145736 | tf_op jit(solution)/shard_map/ppermute | solution.py:19
  19.5 26.5 %collective-permute-start.2 = (bf16[2,16,16,256]{3,2,1,0:T(8,128)(2,1)}, bf16[2,16,16,256]{3,2,1,0:T(8,128)(2,1)S(1)}, u32[]{:S(2)}, u32[]{:S(2)}) collective-permute-start(bf16[2,16,16,256]{3,2,1,0:T(8,128)(2,1)} %slice.379), channel_id=1, source_target_pairs={{1,0},{2,1},{3,2},{4,3},{5,4},{6,5},{7,6},{9,8},{10,9},{11,10},{12... | collective-permute-start | bytes 786440 | tf_op jit(solution)/shard_map/ppermute | solution.py:19
  24.0 91.9 %copy-start.2 = (bf16[8,16,16,256]{3,2,1,0:T(8,128)(2,1)}, bf16[8,16,16,256]{3,2,1,0:T(8,128)(2,1)S(1)}, u32[]{:S(2)}) copy-start(bf16[8,16,16,256]{3,2,1,0:T(8,128)(2,1)S(1)} %gather_fusion) | copy-start | bytes 3145732
  53.3 2.5 copy-start.4
  53.3 2.5 copy-start.12
  56.3 1.2 copy-start.45
  57.5 1.2 copy-start.43
  59.3 1.2 copy-start.40
  60.6 1.2 copy-start.39
  61.8 1.2 copy-start.38
  63.0 1.2 copy-start.37
  64.2 1.2 copy-start.36
  65.5 1.2 copy-start.34
  66.7 1.2 copy-start.32
  67.9 1.2 copy-start.30
  69.6 1.2 copy-start.28
  70.8 1.2 copy-start.26
  72.1 1.2 copy-start.24
  73.3 1.2 copy-start.22
  74.5 1.2 copy-start.20
  75.7 1.2 copy-start.18
  77.0 1.2 copy-start.16
  80.6 1.2 copy-start.14
  83.6 32.3 %copy-start.50 = (f32[256]{0:T(256)S(1)}, f32[256]{0:T(256)}, u32[]{:S(2)}) copy-start(f32[256]{0:T(256)} %param.13) | copy-start | bytes 3076
  83.6 32.3 %copy-start.52 = (f32[256]{0:T(256)S(1)}, f32[256]{0:T(256)}, u32[]{:S(2)}) copy-start(f32[256]{0:T(256)} %param.14) | copy-start | bytes 3076
  120.7 6.6 %collective-permute-start.1 = (bf16[2,16,16,256]{3,2,1,0:T(8,128)(2,1)S(1)}, bf16[2,16,16,256]{3,2,1,0:T(8,128)(2,1)S(1)}, u32[]{:S(2)}, u32[]{:S(2)}) collective-permute-start(bf16[2,16,16,256]{3,2,1,0:T(8,128)(2,1)S(1)} %slice.374), channel_id=1, source_target_pairs={{0,1},{1,2},{2,3},{3,4},{4,5},{5,6},{6,7},{8,9},{9,10},{10,11},{11... | collective-permute-start | bytes 786440 | tf_op jit(solution)/shard_map/ppermute | solution.py:19
  127.3 15.5 %copy-start.48 = (bf16[2,16,16,256]{3,2,1,0:T(8,128)(2,1)}, bf16[2,16,16,256]{3,2,1,0:T(8,128)(2,1)S(1)}, u32[]{:S(2)}) copy-start(bf16[2,16,16,256]{3,2,1,0:T(8,128)(2,1)S(1)} %collective-permute-done.1) | copy-start | bytes 786436
  159.5 110.1 %copy-start.3 = (bf16[8,16,16,256]{3,2,1,0:T(8,128)(2,1)S(1)}, bf16[8,16,16,256]{3,2,1,0:T(8,128)(2,1)}, u32[]{:S(2)}) copy-start(bf16[8,16,16,256]{3,2,1,0:T(8,128)(2,1)} %copy-done.2) | copy-start | bytes 3145732
  159.5 356.1 %all-reduce.9.cloned.1.call-start = ((), (), s32[]{:S(2)}) async-start(), calls=%async_computation.1 | async-start | bytes 14155776 | tf_op jit(solution)/shard_map/psum | solution.py:13
  269.6 4.0 copy-start.49
  285.8 1.5 copy-start.47
  287.3 1.4 copy-start.46
  290.1 1.5 copy-start.44
  291.6 1.4 copy-start.42
  293.0 1.4 copy-start.41
  333.3 2.4 copy-start.5
  333.3 2.6 copy-start.35
  336.0 1.2 copy-start.33
  337.2 1.2 copy-start.31
  338.4 1.2 copy-start.29
  339.6 1.2 copy-start.11
  340.9 1.2 copy-start.27
  342.1 1.2 copy-start.25
  343.3 1.3 copy-start.23
  344.6 1.2 copy-start.21
  345.8 1.2 copy-start.19
  347.0 1.2 copy-start.17
  348.3 1.2 copy-start.15
  349.5 1.2 copy-start.10
  351.2 1.2 copy-start.9
  352.4 1.2 copy-start.8
  353.6 1.2 copy-start.7
  354.9 1.2 copy-start.13
  515.6 6.8 %copy-start.1 = (bf16[1,8,16,16,256]{4,3,2,1,0:T(8,128)(2,1)S(1)}, bf16[1,8,16,16,256]{4,3,2,1,0:T(8,128)(2,1)}, u32[]{:S(2)}) copy-start(bf16[1,8,16,16,256]{4,3,2,1,0:T(8,128)(2,1)} %param.9) | copy-start | bytes 3145732
Sparse Core Ops, SparseCore 0:
  159.6 173.6 all-reduce.6
  335.8 179.6 all-reduce.8
